TPU v7x, 512 devices: a whole 4x8x8 slice. The times are simulated.
512 devices in a mesh: seq: 32 (over x, y), chan: 16 (over z, core).
Axes of the slice: x: 4, y: 8, z: 8, core: 2. Of those that a mesh axis runs over, the one named last changes fastest.
Arguments:
- tokens: bfloat16 [1536, 16384], P('chan', 'seq'), may hold values from -6 to 6
- gate_weight: bfloat16 [1536, 1536], P('chan'), may hold values from -0.15625 to 0.15625
- value_weight: bfloat16 [1536, 1536], P('chan'), may hold values from -0.15625 to 0.15625
- first_factor: bfloat16 [64, 256, 256], P('seq'), may hold values from -0.375 to 0.375
- second_factor: bfloat16 [256, 64, 64], P('seq'), may hold values from -0.75 to 0.75
- down_latent: bfloat16 [1536, 128], P('chan'), may hold values from -0.15625 to 0.15625
- up_latent: bfloat16 [1536, 128], P('chan'), may hold values from -0.5 to 0.5
- doc_lengths: int32 [64], replicated, may hold values from 1 to 8704, 16384 in all
- cotangent: bfloat16 [1536, 16384], P('chan', 'seq'), may hold values from -6 to 6
Outputs:
- hidden: bfloat16 [1536, 16384], P('chan', 'seq')
- d_gate_weight: float32 [1536, 1536], P('chan')
- d_value_weight: float32 [1536, 1536], P('chan')
- d_first: float32 [64, 256, 256], P('seq', 'chan')
- d_second: float32 [256, 64, 64], P('seq', 'chan')
- d_down: float32 [1536, 128], P('chan')
- d_up: float32 [1536, 128], P('chan')
Inputs may be any that keep to these rules, and one draw needn't show every extreme that they name: `doc_lengths`: the documents' lengths sum to 16384; the longest is exactly 8704 tokens.
All inputs are finite; a program needn't handle non-finite values.
Results may differ from a plain program's by a relative error of at most 0.0058.
Values may be sent and summed in bfloat16 or wider, within the bound.
No kernel may reach another device: no remote copies, remote signals or barrier semaphores. Data moves between devices by JAX's collectives and lax.ppermute only.
A program may use at most 64 MiB of HBM per device.

v0:
```python
import jax
import jax.numpy as jnp
from jax import lax
from jax.sharding import PartitionSpec as P

HIGHEST = lax.Precision.HIGHEST


def seq_exchange(x):
    return lax.all_to_all(x, "seq", 0, 0, tiled=True)


def chan_exchange(x):
    return lax.all_to_all(x, "chan", 0, 0, tiled=True)


def body(
    tokens,
    gate_weight,
    value_weight,
    first_factor,
    second_factor,
    down_latent,
    up_latent,
    doc_lengths,
    cotangent,
):
    n_seq = lax.axis_size("seq")
    n_chan = lax.axis_size("chan")
    chan_rows, tok_cols = tokens.shape
    blocks_here, block_width, _ = first_factor.shape
    k_here, n_blk2, _ = second_factor.shape
    lat = down_latent.shape[1]
    n_doc = doc_lengths.shape[0]
    docs_here = n_doc // n_seq
    me = lax.axis_index("seq")
    packed = jnp.concatenate([tokens, down_latent], axis=1)
    gathered_all = lax.all_gather(packed, "chan", axis=0, tiled=True)
    gathered = gathered_all[:, :tok_cols]
    down_full = gathered_all[:, tok_cols:]
    doc_ends = jnp.cumsum(doc_lengths)
    doc_begins = doc_ends - doc_lengths
    position = me * tok_cols + jnp.arange(tok_cols, dtype=jnp.int32)
    member = (
        (position[None, :] >= doc_begins[:, None]) & (position[None, :] < doc_ends[:, None])
    ).astype(jnp.float32)
    len_scale = lax.rsqrt(doc_lengths.astype(jnp.float32))
    gate_pre = jnp.dot(gate_weight, gathered, preferred_element_type=jnp.float32)
    value_bf = jnp.dot(value_weight, gathered, preferred_element_type=jnp.float32).astype(
        jnp.bfloat16
    )
    latent = jnp.einsum("ct,cl->lt", gathered, down_full, preferred_element_type=jnp.float32)
    doc_lat_part = jnp.einsum("dt,lt->dl", member, latent, precision=HIGHEST)
    xdoc_part = jnp.einsum(
        "ct,dt->cd", tokens, member.astype(jnp.bfloat16), preferred_element_type=jnp.float32
    )
    blocked = value_bf.reshape(chan_rows, blocks_here, block_width)
    inner_mix = jnp.einsum(
        "ikj,cij->ikc", first_factor, blocked, preferred_element_type=jnp.float32
    ).astype(jnp.bfloat16)
    sig = jax.nn.sigmoid(gate_pre)
    act = gate_pre * sig
    upstream = cotangent.astype(jnp.float32)
    d_mixed = upstream * act
    d_mixed_bf = d_mixed.astype(jnp.bfloat16)
    per_doc_part = jnp.einsum("ct,dt->cd", d_mixed, member, precision=HIGHEST)
    inner_send = inner_mix.reshape(blocks_here, n_seq, k_here, chan_rows).transpose(1, 0, 2, 3)
    d_send = d_mixed_bf.reshape(chan_rows, blocks_here, n_seq, k_here).transpose(2, 1, 3, 0)
    recv2 = seq_exchange(jnp.concatenate([inner_send, d_send], axis=3))
    columns = recv2[..., :chan_rows].reshape(n_seq * blocks_here, k_here, chan_rows)
    d_outer = recv2[..., chan_rows:].reshape(n_seq * blocks_here, k_here, chan_rows)
    small_send = jnp.concatenate(
        [
            doc_lat_part.reshape(n_seq, docs_here * lat),
            per_doc_part.reshape(chan_rows, n_seq, docs_here)
            .transpose(1, 0, 2)
            .reshape(n_seq, chan_rows * docs_here),
            xdoc_part.reshape(chan_rows, n_seq, docs_here)
            .transpose(1, 0, 2)
            .reshape(n_seq, chan_rows * docs_here),
        ],
        axis=1,
    )
    small_red = jnp.sum(seq_exchange(small_send), axis=0)
    n_a = docs_here * lat
    n_b = chan_rows * docs_here
    scale_here = lax.dynamic_slice(len_scale, (me * docs_here,), (docs_here,))
    pooled_here = small_red[:n_a].reshape(docs_here, lat) * scale_here[:, None]
    per_doc_here = small_red[n_a : n_a + n_b].reshape(chan_rows, docs_here)
    xdoc_here = small_red[n_a + n_b :].reshape(chan_rows, docs_here)
    up_float = up_latent.astype(jnp.float32)
    g_part = jnp.einsum("cd,cl->dl", per_doc_here, up_float, precision=HIGHEST)
    g_here = jnp.sum(chan_exchange(jnp.broadcast_to(g_part.reshape(1, n_a), (n_chan, n_a))), axis=0)
    outer_mix = jnp.einsum(
        "kmi,ikc->mkc", second_factor, columns, preferred_element_type=jnp.float32
    ).astype(jnp.bfloat16)
    d_inner = jnp.einsum(
        "kmi,mkc->ikc", second_factor, d_outer, preferred_element_type=jnp.float32
    ).astype(jnp.bfloat16)
    d_second_part = jnp.einsum("mkc,ikc->kmi", d_outer, columns, preferred_element_type=jnp.float32)
    outer_send = outer_mix.reshape(n_seq, blocks_here, k_here, chan_rows)
    dinner_send = d_inner.reshape(n_seq, blocks_here, k_here, chan_rows)
    recv3 = seq_exchange(jnp.concatenate([outer_send, dinner_send], axis=3))
    outer_tok = (
        recv3[..., :chan_rows]
        .transpose(3, 1, 0, 2)
        .reshape(chan_rows, tok_cols)
        .astype(jnp.float32)
    )
    d_rows = (
        recv3[..., chan_rows:].transpose(1, 0, 2, 3).reshape(blocks_here, n_seq * k_here, chan_rows)
    )
    piece = jnp.concatenate(
        [pooled_here.reshape(n_a), per_doc_here.reshape(n_b), xdoc_here.reshape(n_b)]
    )
    gath3 = seq_exchange(jnp.broadcast_to(piece[None, :], (n_seq, piece.shape[0])))
    pooled = gath3[:, :n_a].reshape(n_doc, lat)
    per_doc = (
        gath3[:, n_a : n_a + n_b]
        .reshape(n_seq, chan_rows, docs_here)
        .transpose(1, 0, 2)
        .reshape(chan_rows, n_doc)
    )
    xdoc = (
        gath3[:, n_a + n_b :]
        .reshape(n_seq, chan_rows, docs_here)
        .transpose(1, 0, 2)
        .reshape(chan_rows, n_doc)
    )
    spread = jnp.einsum("dl,cl->cd", pooled, up_float, precision=HIGHEST)
    summary = jnp.dot(spread, member, precision=HIGHEST)
    mixed = outer_tok + summary
    hidden = (act * mixed).astype(jnp.bfloat16)
    d_gate_bf = (upstream * mixed * sig * (1.0 + gate_pre * (1.0 - sig))).astype(jnp.bfloat16)
    d_value_bf = (
        jnp.einsum("ikj,ikc->cij", first_factor, d_rows, preferred_element_type=jnp.float32)
        .astype(jnp.bfloat16)
        .reshape(chan_rows, tok_cols)
    )
    d_first_part = jnp.einsum("ikc,cij->ikj", d_rows, blocked, preferred_element_type=jnp.float32)
    d_up = jnp.einsum("cd,dl->cl", per_doc, pooled, precision=HIGHEST)
    both_grads = jnp.concatenate([d_gate_bf, d_value_bf], axis=0)
    d_proj_part = jnp.einsum("ot,it->oi", both_grads, gathered, preferred_element_type=jnp.float32)
    rows_here = 2 * chan_rows // n_seq
    width = d_proj_part.shape[1]
    proj_red = jnp.sum(seq_exchange(d_proj_part.reshape(n_seq, rows_here, width)), axis=0)
    k_part = block_width // n_chan
    m_part = n_blk2 // n_chan
    first_send = (
        d_first_part.reshape(blocks_here, n_chan, k_part, block_width)
        .transpose(1, 0, 2, 3)
        .reshape(n_chan, -1)
    )
    second_send = (
        d_second_part.reshape(k_here, n_chan, m_part, n_blk2)
        .transpose(1, 0, 2, 3)
        .reshape(n_chan, -1)
    )
    fac_red = jnp.sum(chan_exchange(jnp.concatenate([first_send, second_send], axis=1)), axis=0)
    n_f = blocks_here * k_part * block_width
    d_first = fac_red[:n_f].reshape(blocks_here, k_part, block_width)
    d_second = fac_red[n_f:].reshape(k_here, m_part, n_blk2)
    piece5 = jnp.concatenate([proj_red.reshape(-1), g_here])
    gath5 = seq_exchange(jnp.broadcast_to(piece5[None, :], (n_seq, piece5.shape[0])))
    n_p = rows_here * width
    d_proj = gath5[:, :n_p].reshape(2 * chan_rows, width)
    d_pooled = gath5[:, n_p:].reshape(n_doc, lat) * len_scale[:, None]
    d_down = jnp.einsum(
        "cd,dl->cl", xdoc, d_pooled.astype(jnp.bfloat16).astype(jnp.float32), precision=HIGHEST
    )
    return (hidden, d_proj[:chan_rows], d_proj[chan_rows:], d_first, d_second, d_down, d_up)


def solution(mesh):
    in_specs = (
        P("chan", "seq"),
        P("chan", None),
        P("chan", None),
        P("seq", None, None),
        P("seq", None, None),
        P("chan", None),
        P("chan", None),
        P(),
        P("chan", "seq"),
    )
    out_specs = (
        P("chan", "seq"),
        P("chan", None),
        P("chan", None),
        P("seq", "chan", None),
        P("seq", "chan", None),
        P("chan", None),
        P("chan", None),
    )
    return jax.shard_map(body, mesh=mesh, in_specs=in_specs, out_specs=out_specs, check_vma=False)
```

profile of v0, /device:TPU:1, one launch (start us, length us, event | category | flops | bytes accessed | tf_op | source)
XLA Modules:
  0.0 258.2 jit_solution(9266337359368972084)
XLA Ops:
  7.2 1.6 pad_maximum_fusion.2
  8.9 0.7 copy.140
  9.8 0.7 sub.6
  10.5 1.1 fusion.27
  11.8 47.7 %all-gather.2.cloned.1.call-done = bf16[1536,640]{1,0:T(8,128)(2,1)} async-done(((bf16[96,640]{1,0:T(8,128)(2,1)}), bf16[1536,640]{1,0:T(8,128)(2,1)}) %all-gather.2.cloned.1.call-update) | async-done | bytes 1966096 | tf_op jit(solution)/shard_map/all_gather | solution.py:38
  59.4 2.1 fusion.4
  61.5 0.3 fusion.31
  61.8 0.4 fusion.17
  62.3 0.3 fusion.16
  62.7 0.2 copy-done.17
  63.1 0.7 all_to_all.39
  63.8 9.3 %all-to-all-start.2 = ((f32[32,1,640]{2,1,0:T(1,128)}), f32[32,1,640]{2,1,0:T(1,128)S(1)}, u32[]{:S(2)}, u32[]{:S(2)}) async-start(f32[32,1,640]{2,1,0:T(1,128)} %all_to_all.39), calls=%async_computation.2 | async-start | bytes 163840 | tf_op jit(solution)/shard_map/all_to_all | solution.py:10
  73.1 1.3 convolution_convert_fusion.2
  74.4 0.2 fusion
  74.7 0.1 copy.131
  74.8 0.3 copy-done.10
  75.2 0.1 pad_maximum_fusion
  75.3 0.7 copy.133
  76.0 6.0 %all-to-all-done.2 = f32[32,1,640]{2,1,0:T(1,128)S(1)} async-done(((f32[32,1,640]{2,1,0:T(1,128)}), f32[32,1,640]{2,1,0:T(1,128)S(1)}, u32[]{:S(2)}, u32[]{:S(2)}) %all-to-all-start.2) | async-done | bytes 81952 | tf_op jit(solution)/shard_map/all_to_all | solution.py:10
  82.0 3.9 %all-to-all-start = ((bf16[32,2,8,192]{3,2,1,0:T(8,128)(2,1)}), bf16[32,2,8,192]{3,2,1,0:T(8,128)(2,1)S(1)}, u32[]{:S(2)}, u32[]{:S(2)}) async-start(bf16[32,2,8,192]{3,2,1,0:T(8,128)(2,1)} %copy.133), calls=%async_computation | async-start | bytes 524288 | tf_op jit(solution)/shard_map/all_to_all | solution.py:10
  86.0 0.4 copy-done.14
  86.6 9.0 %all-to-all-done = bf16[32,2,8,192]{3,2,1,0:T(8,128)(2,1)S(1)} async-done(((bf16[32,2,8,192]{3,2,1,0:T(8,128)(2,1)}), bf16[32,2,8,192]{3,2,1,0:T(8,128)(2,1)S(1)}, u32[]{:S(2)}, u32[]{:S(2)}) %all-to-all-start) | async-done | bytes 196640 | tf_op jit(solution)/shard_map/all_to_all | solution.py:10
  95.5 0.7 broadcast_in_dim.8
  96.2 6.2 %all-to-all-start.3 = ((f32[32,1,640]{2,1,0:T(1,128)}), f32[32,1,640]{2,1,0:T(1,128)S(1)}, u32[]{:S(2)}, u32[]{:S(2)}) async-start(f32[32,1,640]{2,1,0:T(1,128)} %broadcast_in_dim.8), calls=%async_computation.3 | async-start | bytes 163840 | tf_op jit(solution)/shard_map/all_to_all | solution.py:10
  102.8 0.5 copy-done.2
  103.4 0.2 convolution_convert_fusion
  103.5 0.2 convolution_convert_fusion.1
  103.8 0.2 copy.137
  103.9 0.2 copy.138
  104.1 0.8 pad_maximum_fusion.1
  105.0 6.4 %all-to-all-done.3 = f32[32,1,640]{2,1,0:T(1,128)S(1)} async-done(((f32[32,1,640]{2,1,0:T(1,128)}), f32[32,1,640]{2,1,0:T(1,128)S(1)}, u32[]{:S(2)}, u32[]{:S(2)}) %all-to-all-start.3) | async-done | bytes 81952 | tf_op jit(solution)/shard_map/all_to_all | solution.py:10
  111.4 3.9 %all-to-all-start.1 = ((bf16[32,2,8,192]{3,2,1,0:T(8,128)(2,1)}), bf16[32,2,8,192]{3,2,1,0:T(8,128)(2,1)S(1)}, u32[]{:S(2)}, u32[]{:S(2)}) async-start(bf16[32,2,8,192]{3,2,1,0:T(8,128)(2,1)} %pad_maximum_fusion.1), calls=%async_computation.1 | async-start | bytes 524288 | tf_op jit(solution)/shard_map/all_to_all | solution.py:10
  115.3 0.1 reshape.211
  115.4 0.2 convolution_bitcast_fusion.1
  115.7 0.2 fusion.36
  115.8 9.2 %all-to-all-done.1 = bf16[32,2,8,192]{3,2,1,0:T(8,128)(2,1)S(1)} async-done(((bf16[32,2,8,192]{3,2,1,0:T(8,128)(2,1)}), bf16[32,2,8,192]{3,2,1,0:T(8,128)(2,1)S(1)}, u32[]{:S(2)}, u32[]{:S(2)}) %all-to-all-start.1) | async-done | bytes 196640 | tf_op jit(solution)/shard_map/all_to_all | solution.py:10
  125.0 0.6 broadcast_in_dim.10
  125.6 8.4 %all-to-all-start.5 = ((f32[16,1,256]{2,1,0:T(1,128)}), f32[16,1,256]{2,1,0:T(1,128)}, u32[]{:S(2)}, u32[]{:S(2)}) async-start(f32[16,1,256]{2,1,0:T(1,128)} %broadcast_in_dim.10), calls=%async_computation.5 | async-start | bytes 32768 | tf_op jit(solution)/shard_map/all_to_all | solution.py:14
  134.3 0.2 fusion.1
  134.5 1.9 fusion.11
  136.4 0.7 fusion.2
  137.1 1.3 reshape.209
  138.4 2.9 %all-to-all-done.5 = f32[16,1,256]{2,1,0:T(1,128)} async-done(((f32[16,1,256]{2,1,0:T(1,128)}), f32[16,1,256]{2,1,0:T(1,128)}, u32[]{:S(2)}, u32[]{:S(2)}) %all-to-all-start.5) | async-done | bytes 16416 | tf_op jit(solution)/shard_map/all_to_all | solution.py:14
  141.3 4.2 %all-to-all-start.4 = ((f32[32,6,1536]{2,1,0:T(8,128)}), f32[32,6,1536]{2,1,0:T(8,128)S(1)}, u32[]{:S(2)}, u32[]{:S(2)}) async-start(f32[32,6,1536]{2,1,0:T(8,128)} %reshape.209), calls=%async_computation.4 | async-start | bytes 3145728 | tf_op jit(solution)/shard_map/all_to_all | solution.py:10
  145.6 0.2 fusion.37
  145.8 0.2 reshape.215
  146.1 0.2 fusion.18
  146.4 0.3 copy.167
  146.7 1.5 copy.154
  148.2 33.8 %all-to-all-done.4 = f32[32,6,1536]{2,1,0:T(8,128)S(1)} async-done(((f32[32,6,1536]{2,1,0:T(8,128)}), f32[32,6,1536]{2,1,0:T(8,128)S(1)}, u32[]{:S(2)}, u32[]{:S(2)}) %all-to-all-start.4) | async-done | bytes 1179680 | tf_op jit(solution)/shard_map/all_to_all | solution.py:10
  182.1 7.8 %all-to-all-start.7 = ((f32[16,1,10240]{2,1,0:T(1,128)}), f32[16,1,10240]{2,1,0:T(1,128)S(1)}, u32[]{:S(2)}, u32[]{:S(2)}) async-start(f32[16,1,10240]{2,1,0:T(1,128)} %copy.154), calls=%async_computation.7 | async-start | bytes 1310720 | tf_op jit(solution)/shard_map/all_to_all | solution.py:14
  189.9 0.8 reduce_sum.38
  190.7 0.1 reduce_sum.37
  190.8 19.0 %all-to-all-done.7 = f32[16,1,10240]{2,1,0:T(1,128)S(1)} async-done(((f32[16,1,10240]{2,1,0:T(1,128)}), f32[16,1,10240]{2,1,0:T(1,128)S(1)}, u32[]{:S(2)}, u32[]{:S(2)}) %all-to-all-start.7) | async-done | bytes 655392 | tf_op jit(solution)/shard_map/all_to_all | solution.py:14
  209.9 1.7 broadcast_in_dim.11
  211.5 5.3 %all-to-all-start.6 = ((f32[32,1,9472]{2,1,0:T(1,128)}), f32[32,1,9472]{2,1,0:T(1,128)S(1)}, u32[]{:S(2)}, u32[]{:S(2)}) async-start(f32[32,1,9472]{2,1,0:T(1,128)} %broadcast_in_dim.11), calls=%async_computation.6 | async-start | bytes 2424832 | tf_op jit(solution)/shard_map/all_to_all | solution.py:10
  217.5 0.9 fusion.39
  218.4 0.4 reduce_sum.39
  218.8 0.6 reshape.216
  219.4 0.7 reshape.217
  220.1 28.2 %all-to-all-done.6 = f32[32,1,9472]{2,1,0:T(1,128)S(1)} async-done(((f32[32,1,9472]{2,1,0:T(1,128)}), f32[32,1,9472]{2,1,0:T(1,128)S(1)}, u32[]{:S(2)}, u32[]{:S(2)}) %all-to-all-start.6) | async-done | bytes 1212448 | tf_op jit(solution)/shard_map/all_to_all | solution.py:10
  248.6 0.9 slice.101
  249.5 0.9 slice.99
  250.5 0.9 fusion.38
  (79 shorter events, 2.7 us)
Async XLA Ops:
  7.2 54.6 %copy-start = (bf16[96,1536]{1,0:T(8,128)(2,1)S(1)}, bf16[96,1536]{1,0:T(8,128)(2,1)}, u32[]{:S(2)}) copy-start(bf16[96,1536]{1,0:T(8,128)(2,1)} %param.10) | copy-start | bytes 884740
  7.2 52.2 %all-gather.2.cloned.1.call-start = ((), (), s32[]{:S(2)}) async-start(), calls=%async_computation.8 | async-start | bytes 2088960 | tf_op jit(solution)/shard_map/all_gather | solution.py:38
  9.7 52.1 %copy-start.16 = (bf16[96,512]{1,0:T(8,128)(2,1)S(1)}, bf16[96,512]{1,0:T(8,128)(2,1)}, u32[]{:S(2)}) copy-start(bf16[96,512]{1,0:T(8,128)(2,1)} %param.17) | copy-start | bytes 294916
  59.4 2.4 copy-start.1
  62.3 0.7 copy-start.17
  62.6 11.8 %copy-start.8 = (bf16[2,256,256]{2,1,0:T(8,128)(2,1)S(1)}, bf16[2,256,256]{2,1,0:T(8,128)(2,1)}, u32[]{:S(2)}) copy-start(bf16[2,256,256]{2,1,0:T(8,128)(2,1)} %param.12) | copy-start | bytes 786436
  63.8 18.2 %all-to-all-start.2 = ((f32[32,1,640]{2,1,0:T(1,128)}), f32[32,1,640]{2,1,0:T(1,128)S(1)}, u32[]{:S(2)}, u32[]{:S(2)}) async-start(f32[32,1,640]{2,1,0:T(1,128)} %all_to_all.39), calls=%async_computation.2 | async-start | bytes 163840 | tf_op jit(solution)/shard_map/all_to_all | solution.py:10
  74.4 0.6 copy-start.10
  74.4 11.5 %copy-start.13 = (s32[64]{0:T(128)S(1)}, s32[64]{0:T(128)}, u32[]{:S(2)}) copy-start(s32[64]{0:T(128)} %param.16) | copy-start | bytes 772
  75.0 28.3 %copy-start.9 = (bf16[8,64,64]{2,1,0:T(8,128)(2,1)S(1)}, bf16[8,64,64]{2,1,0:T(8,128)(2,1)}, u32[]{:S(2)}) copy-start(bf16[8,64,64]{2,1,0:T(8,128)(2,1)} %param.13) | copy-start | bytes 196612
  82.0 13.5 %all-to-all-start = ((bf16[32,2,8,192]{3,2,1,0:T(8,128)(2,1)}), bf16[32,2,8,192]{3,2,1,0:T(8,128)(2,1)S(1)}, u32[]{:S(2)}, u32[]{:S(2)}) async-start(bf16[32,2,8,192]{3,2,1,0:T(8,128)(2,1)} %copy.133), calls=%async_computation | async-start | bytes 524288 | tf_op jit(solution)/shard_map/all_to_all | solution.py:10
  85.9 0.5 copy-start.14
  96.2 15.2 %all-to-all-start.3 = ((f32[32,1,640]{2,1,0:T(1,128)}), f32[32,1,640]{2,1,0:T(1,128)S(1)}, u32[]{:S(2)}, u32[]{:S(2)}) async-start(f32[32,1,640]{2,1,0:T(1,128)} %broadcast_in_dim.8), calls=%async_computation.3 | async-start | bytes 163840 | tf_op jit(solution)/shard_map/all_to_all | solution.py:10
  102.6 12.8 %copy-start.12 = (bf16[96,128]{1,0:T(8,128)(2,1)S(1)}, bf16[96,128]{1,0:T(8,128)(2,1)}, u32[]{:S(2)}) copy-start(bf16[96,128]{1,0:T(8,128)(2,1)} %param.15) | copy-start | bytes 73732
  102.7 0.7 copy-start.2
  102.8 0.7 copy-start.4
  111.4 13.6 %all-to-all-start.1 = ((bf16[32,2,8,192]{3,2,1,0:T(8,128)(2,1)}), bf16[32,2,8,192]{3,2,1,0:T(8,128)(2,1)S(1)}, u32[]{:S(2)}, u32[]{:S(2)}) async-start(bf16[32,2,8,192]{3,2,1,0:T(8,128)(2,1)} %pad_maximum_fusion.1), calls=%async_computation.1 | async-start | bytes 524288 | tf_op jit(solution)/shard_map/all_to_all | solution.py:10
  125.6 15.7 %all-to-all-start.5 = ((f32[16,1,256]{2,1,0:T(1,128)}), f32[16,1,256]{2,1,0:T(1,128)}, u32[]{:S(2)}, u32[]{:S(2)}) async-start(f32[16,1,256]{2,1,0:T(1,128)} %broadcast_in_dim.10), calls=%async_computation.5 | async-start | bytes 32768 | tf_op jit(solution)/shard_map/all_to_all | solution.py:14
  134.1 2.3 copy-start.6
  138.4 7.1 %copy-start.3 = (bf16[32,2,8,96]{3,1,0,2:T(2,128)(2,1)S(1)}, bf16[32,2,8,96]{3,1,0,2:T(2,128)(2,1)}, u32[]{:S(2)}) copy-start(bf16[32,2,8,96]{3,1,0,2:T(2,128)(2,1)} %copy-done.2) | copy-start | bytes 294916
  138.4 7.1 %copy-start.5 = (bf16[32,2,8,96]{3,1,0,2:T(2,128)(2,1)S(1)}, bf16[32,2,8,96]{3,1,0,2:T(2,128)(2,1)}, u32[]{:S(2)}) copy-start(bf16[32,2,8,96]{3,1,0,2:T(2,128)(2,1)} %copy-done.4) | copy-start | bytes 294916
  138.4 7.6 %copy-start.7 = (bf16[2,32,8,96]{3,2,0,1:T(8,128)(2,1)S(1)}, bf16[2,32,8,96]{3,2,0,1:T(8,128)(2,1)}, u32[]{:S(2)}) copy-start(bf16[2,32,8,96]{3,2,0,1:T(8,128)(2,1)} %copy-done.6) | copy-start | bytes 294916
  138.4 7.6 %copy-start.11 = (bf16[512,96]{0,1:T(8,128)(2,1)S(1)}, bf16[512,96]{0,1:T(8,128)(2,1)}, u32[]{:S(2)}) copy-start(bf16[512,96]{0,1:T(8,128)(2,1)} %copy-done.10) | copy-start | bytes 294916
  141.3 40.7 %all-to-all-start.4 = ((f32[32,6,1536]{2,1,0:T(8,128)}), f32[32,6,1536]{2,1,0:T(8,128)S(1)}, u32[]{:S(2)}, u32[]{:S(2)}) async-start(f32[32,6,1536]{2,1,0:T(8,128)} %reshape.209), calls=%async_computation.4 | async-start | bytes 3145728 | tf_op jit(solution)/shard_map/all_to_all | solution.py:10
  182.1 27.8 %all-to-all-start.7 = ((f32[16,1,10240]{2,1,0:T(1,128)}), f32[16,1,10240]{2,1,0:T(1,128)S(1)}, u32[]{:S(2)}, u32[]{:S(2)}) async-start(f32[16,1,10240]{2,1,0:T(1,128)} %copy.154), calls=%async_computation.7 | async-start | bytes 1310720 | tf_op jit(solution)/shard_map/all_to_all | solution.py:14
  190.8 26.1 %copy-start.15 = (f32[64]{0:T(128)S(1)}, f32[64]{0:T(128)}, u32[]{:S(2)}) copy-start(f32[64]{0:T(128)} %copy-done.14) | copy-start | bytes 772
  211.5 36.8 %all-to-all-start.6 = ((f32[32,1,9472]{2,1,0:T(1,128)}), f32[32,1,9472]{2,1,0:T(1,128)S(1)}, u32[]{:S(2)}, u32[]{:S(2)}) async-start(f32[32,1,9472]{2,1,0:T(1,128)} %broadcast_in_dim.11), calls=%async_computation.6 | async-start | bytes 2424832 | tf_op jit(solution)/shard_map/all_to_all | solution.py:10
Sparse Core Ops, SparseCore 0:
  10.7 48.6 all-gather.1
where the time goes:
time: 259 us; the launch traced here: 258 us
  waiting for transfers between devices  162 us (63%)
  starting transfers between devices  49 us (19%)
  local copies, waits for them, and re-layouts  15.8 us (6%)
  between operations  14.6 us (6%)
  matrix products  11.5 us (4%)
  other arithmetic  5.15 us (2%)
    all_to_all x6, waiting for transfers between devices, seq_exchange(): return lax.all_to_all(x, 'seq', 0, 0, tiled=True)  92.6 us
    all_gather x1, waiting for transfers between devices, body(): gathered_all = lax.all_gather(packed, 'chan', axis=0, tiled=True)  47.7 us
    all_to_all x6, starting transfers between devices, seq_exchange(): return lax.all_to_all(x, 'seq', 0, 0, tiled=True)  32.8 us
    all_to_all x2, waiting for transfers between devices, chan_exchange(): return lax.all_to_all(x, 'chan', 0, 0, tiled=True)  21.9 us
    all_to_all x2, starting transfers between devices, chan_exchange(): return lax.all_to_all(x, 'chan', 0, 0, tiled=True)  16.2 us
  transfers between devices with their start and end apart: 9, of which 9 were waited for; matrix products, arithmetic and copies ran while one was open for 7% of the time, Pallas kernels for 0%

commit v1 on v0

--- a/solution.py
+++ b/solution.py
@@ -35,7 +35,22 @@
     docs_here = n_doc // n_seq
     me = lax.axis_index("seq")
     packed = jnp.concatenate([tokens, down_latent], axis=1)
-    gathered_all = lax.all_gather(packed, "chan", axis=0, tiled=True)
+    size, mine, rows = (lax.axis_size("chan"), lax.axis_index("chan"), packed.shape[0])
+    right = [(i, (i + 1) % size) for i in range(size)]
+    left = [(i, (i - 1) % size) for i in range(size)]
+    out = jnp.zeros((*packed.shape[:0], size * rows, *packed.shape[0 + 1 :]), packed.dtype)
+    out = lax.dynamic_update_slice_in_dim(out, packed, mine * rows, axis=0)
+    from_left = from_right = packed
+    halfway = size // 2
+    for turn in range(1, halfway + 1):
+        from_left = lax.ppermute(from_left, "chan", right)
+        out = lax.dynamic_update_slice_in_dim(out, from_left, (mine - turn) % size * rows, axis=0)
+        if turn < size - halfway:
+            from_right = lax.ppermute(from_right, "chan", left)
+            out = lax.dynamic_update_slice_in_dim(
+                out, from_right, (mine + turn) % size * rows, axis=0
+            )
+    gathered_all = out
     gathered = gathered_all[:, :tok_cols]
     down_full = gathered_all[:, tok_cols:]
     doc_ends = jnp.cumsum(doc_lengths)

time: 259 us -> 246 us (0.950)
  starting transfers between devices: 49 us -> 86.6 us
  waiting for transfers between devices: 162 us -> 125 us
  between operations: 14.6 us -> 1.56 us
    all_gather x1 -> x0, waiting for transfers between devices: 47.7 us -> none  [body(): gathered_all = lax.all_gather(packed, 'chan', axis=0, tiled=True)]
    ppermute x0 -> x15, starting transfers between devices: none -> 32.9 us  [the longest x7 29 us: body(): from_right = lax.ppermute(from_right, 'chan', left)]
    ppermute x0 -> x15, waiting for transfers between devices: none -> 10.7 us  [the longest x8 9.93 us: body(): from_left = lax.ppermute(from_left, 'chan', right)]
    all_to_all x2, starting transfers between devices: 16.2 us -> 22.3 us  [chan_exchange(): return lax.all_to_all(x, 'chan', 0, 0, tiled=True)]
  transfers between devices with their start and end apart: 9 -> 23, of which waited for: 9 -> 20; matrix products, arithmetic and copies ran while one was open for 7% -> 8% of each run, Pallas kernels for 0% -> 0%
where the time goes in v1:
time: 246 us; the launch traced here: 245 us
  waiting for transfers between devices  125 us (51%)
  starting transfers between devices  86.6 us (35%)
  local copies, waits for them, and re-layouts  17.9 us (7%)
  matrix products  9.78 us (4%)
  other arithmetic  3.53 us (1%)
    all_to_all x6, waiting for transfers between devices, seq_exchange(): return lax.all_to_all(x, 'seq', 0, 0, tiled=True)  92.7 us
    all_to_all x6, starting transfers between devices, seq_exchange(): return lax.all_to_all(x, 'seq', 0, 0, tiled=True)  31.5 us
    ppermute x7, starting transfers between devices, body(): from_right = lax.ppermute(from_right, 'chan', left)  29 us
    all_to_all x2, starting transfers between devices, chan_exchange(): return lax.all_to_all(x, 'chan', 0, 0, tiled=True)  22.3 us
    all_to_all x2, waiting for transfers between devices, chan_exchange(): return lax.all_to_all(x, 'chan', 0, 0, tiled=True)  22 us
    ppermute x8, waiting for transfers between devices, body(): from_left = lax.ppermute(from_left, 'chan', right)  9.93 us
  transfers between devices with their start and end apart: 23, of which 20 were waited for; matrix products, arithmetic and copies ran while one was open for 8% of the time, Pallas kernels for 0%

profile of v1, /device:TPU:1, one launch (start us, length us, event | category | flops | bytes accessed | tf_op | source)
XLA Modules:
  0.0 244.8 jit_solution(6766438667517531094)
XLA Ops:
  0.6 0.9 constant_dynamic-update-slice_fusion.1
  1.6 0.7 constant_dynamic-update-slice_fusion
  2.3 3.5 %collective-permute-start = (bf16[96,640]{1,0:T(8,128)(2,1)S(1)}, bf16[96,640]{1,0:T(8,128)(2,1)S(1)}, u32[]{:S(2)}, u32[]{:S(2)}) collective-permute-start(bf16[96,640]{1,0:T(8,128)(2,1)S(1)} %constant_dynamic-update-slice_fusion), channel_id=1, source_target_pairs={{0,1},{1,2},{2,3},{3,4},{4,5},{5,6},{6,7},{7,8},{8,9},{9,10},{10,1... | collective-permute-start | bytes 368648 | tf_op jit(solution)/shard_map/ppermute | solution.py:46
  5.8 3.4 %collective-permute-start.1 = (bf16[96,640]{1,0:T(8,128)(2,1)S(1)}, bf16[96,640]{1,0:T(8,128)(2,1)S(1)}, u32[]{:S(2)}, u32[]{:S(2)}) collective-permute-start(bf16[96,640]{1,0:T(8,128)(2,1)S(1)} %constant_dynamic-update-slice_fusion), channel_id=1, source_target_pairs={{0,15},{1,0},{2,1},{3,2},{4,3},{5,4},{6,5},{7,6},{8,7},{9,8},{10,9... | collective-permute-start | bytes 368648 | tf_op jit(solution)/shard_map/ppermute | solution.py:49
  9.2 0.7 copy.140
  10.1 0.7 sub.38
  10.8 1.1 fusion.27
  12.6 3.1 %collective-permute-start.3 = (bf16[96,640]{1,0:T(8,128)(2,1)S(1)}, bf16[96,640]{1,0:T(8,128)(2,1)S(1)}, u32[]{:S(2)}, u32[]{:S(2)}) collective-permute-start(bf16[96,640]{1,0:T(8,128)(2,1)S(1)} %collective-permute-done.1), channel_id=1, source_target_pairs={{0,15},{1,0},{2,1},{3,2},{4,3},{5,4},{6,5},{7,6},{8,7},{9,8},{10,9... | collective-permute-start | bytes 368648 | tf_op jit(solution)/shard_map/ppermute | solution.py:49
  15.8 0.7 collective-permute-done.2
  16.5 0.3 collective-permute-start.4
  16.9 4.3 %collective-permute-start.5 = (bf16[96,640]{1,0:T(8,128)(2,1)S(1)}, bf16[96,640]{1,0:T(8,128)(2,1)S(1)}, u32[]{:S(2)}, u32[]{:S(2)}) collective-permute-start(bf16[96,640]{1,0:T(8,128)(2,1)S(1)} %collective-permute-done.3), channel_id=1, source_target_pairs={{0,15},{1,0},{2,1},{3,2},{4,3},{5,4},{6,5},{7,6},{8,7},{9,8},{10,9... | collective-permute-start | bytes 368648 | tf_op jit(solution)/shard_map/ppermute | solution.py:49
  21.2 0.8 collective-permute-done.4
  22.2 4.5 %collective-permute-start.7 = (bf16[96,640]{1,0:T(8,128)(2,1)S(1)}, bf16[96,640]{1,0:T(8,128)(2,1)S(1)}, u32[]{:S(2)}, u32[]{:S(2)}) collective-permute-start(bf16[96,640]{1,0:T(8,128)(2,1)S(1)} %collective-permute-done.5), channel_id=1, source_target_pairs={{0,15},{1,0},{2,1},{3,2},{4,3},{5,4},{6,5},{7,6},{8,7},{9,8},{10,9... | collective-permute-start | bytes 368648 | tf_op jit(solution)/shard_map/ppermute | solution.py:49
  26.8 0.8 collective-permute-done.6
  27.7 4.5 %collective-permute-start.9 = (bf16[96,640]{1,0:T(8,128)(2,1)S(1)}, bf16[96,640]{1,0:T(8,128)(2,1)S(1)}, u32[]{:S(2)}, u32[]{:S(2)}) collective-permute-start(bf16[96,640]{1,0:T(8,128)(2,1)S(1)} %collective-permute-done.7), channel_id=1, source_target_pairs={{0,15},{1,0},{2,1},{3,2},{4,3},{5,4},{6,5},{7,6},{8,7},{9,8},{10,9... | collective-permute-start | bytes 368648 | tf_op jit(solution)/shard_map/ppermute | solution.py:49
  32.3 0.8 collective-permute-done.8
  33.2 4.5 %collective-permute-start.11 = (bf16[96,640]{1,0:T(8,128)(2,1)S(1)}, bf16[96,640]{1,0:T(8,128)(2,1)S(1)}, u32[]{:S(2)}, u32[]{:S(2)}) collective-permute-start(bf16[96,640]{1,0:T(8,128)(2,1)S(1)} %collective-permute-done.9), channel_id=1, source_target_pairs={{0,15},{1,0},{2,1},{3,2},{4,3},{5,4},{6,5},{7,6},{8,7},{9,8},{10,9... | collective-permute-start | bytes 368648 | tf_op jit(solution)/shard_map/ppermute | solution.py:49
  37.8 0.8 collective-permute-done.10
  38.7 4.5 %collective-permute-start.13 = (bf16[96,640]{1,0:T(8,128)(2,1)S(1)}, bf16[96,640]{1,0:T(8,128)(2,1)S(1)}, u32[]{:S(2)}, u32[]{:S(2)}) collective-permute-start(bf16[96,640]{1,0:T(8,128)(2,1)S(1)} %collective-permute-done.11), channel_id=1, source_target_pairs={{0,15},{1,0},{2,1},{3,2},{4,3},{5,4},{6,5},{7,6},{8,7},{9,8},{10,9... | collective-permute-start | bytes 368648 | tf_op jit(solution)/shard_map/ppermute | solution.py:49
  43.3 0.8 collective-permute-done.12
  44.3 5.3 %collective-permute-done.14 = bf16[96,640]{1,0:T(8,128)(2,1)S(1)} collective-permute-done((bf16[96,640]{1,0:T(8,128)(2,1)S(1)}, bf16[96,640]{1,0:T(8,128)(2,1)S(1)}, u32[]{:S(2)}, u32[]{:S(2)}) %collective-permute-start.14) | collective-permute-done | bytes 122912 | tf_op jit(solution)/shard_map/ppermute | solution.py:46
  49.6 0.4 fusion.4
  50.0 0.4 fusion.17
  50.5 0.3 fusion.16
  50.8 0.4 copy-done.16
  51.3 0.3 fusion.31
  51.7 0.7 all_to_all.39
  52.4 9.7 %all-to-all-start.2 = ((f32[32,1,640]{2,1,0:T(1,128)}), f32[32,1,640]{2,1,0:T(1,128)S(1)}, u32[]{:S(2)}, u32[]{:S(2)}) async-start(f32[32,1,640]{2,1,0:T(1,128)} %all_to_all.39), calls=%async_computation.2 | async-start | bytes 163840 | tf_op jit(solution)/shard_map/all_to_all | solution.py:10
  62.1 1.3 convolution_convert_fusion.2
  64.2 0.7 copy.133
  65.0 6.1 %all-to-all-done.2 = f32[32,1,640]{2,1,0:T(1,128)S(1)} async-done(((f32[32,1,640]{2,1,0:T(1,128)}), f32[32,1,640]{2,1,0:T(1,128)S(1)}, u32[]{:S(2)}, u32[]{:S(2)}) %all-to-all-start.2) | async-done | bytes 81952 | tf_op jit(solution)/shard_map/all_to_all | solution.py:10
  71.0 3.9 %all-to-all-start = ((bf16[32,2,8,192]{3,2,1,0:T(8,128)(2,1)}), bf16[32,2,8,192]{3,2,1,0:T(8,128)(2,1)S(1)}, u32[]{:S(2)}, u32[]{:S(2)}) async-start(bf16[32,2,8,192]{3,2,1,0:T(8,128)(2,1)} %copy.133), calls=%async_computation | async-start | bytes 524288 | tf_op jit(solution)/shard_map/all_to_all | solution.py:10
  75.1 0.3 copy-done.13
  75.5 9.0 %all-to-all-done = bf16[32,2,8,192]{3,2,1,0:T(8,128)(2,1)S(1)} async-done(((bf16[32,2,8,192]{3,2,1,0:T(8,128)(2,1)}), bf16[32,2,8,192]{3,2,1,0:T(8,128)(2,1)S(1)}, u32[]{:S(2)}, u32[]{:S(2)}) %all-to-all-start) | async-done | bytes 196640 | tf_op jit(solution)/shard_map/all_to_all | solution.py:10
  84.6 0.7 broadcast_in_dim.11
  85.2 4.4 %all-to-all-start.3 = ((f32[32,1,640]{2,1,0:T(1,128)}), f32[32,1,640]{2,1,0:T(1,128)S(1)}, u32[]{:S(2)}, u32[]{:S(2)}) async-start(f32[32,1,640]{2,1,0:T(1,128)} %broadcast_in_dim.11), calls=%async_computation.3 | async-start | bytes 163840 | tf_op jit(solution)/shard_map/all_to_all | solution.py:10
  90.0 0.5 copy-done.1
  91.2 0.8 pad_maximum_fusion.1
  92.1 6.5 %all-to-all-done.3 = f32[32,1,640]{2,1,0:T(1,128)S(1)} async-done(((f32[32,1,640]{2,1,0:T(1,128)}), f32[32,1,640]{2,1,0:T(1,128)S(1)}, u32[]{:S(2)}, u32[]{:S(2)}) %all-to-all-start.3) | async-done | bytes 81952 | tf_op jit(solution)/shard_map/all_to_all | solution.py:10
  98.6 3.9 %all-to-all-start.1 = ((bf16[32,2,8,192]{3,2,1,0:T(8,128)(2,1)}), bf16[32,2,8,192]{3,2,1,0:T(8,128)(2,1)S(1)}, u32[]{:S(2)}, u32[]{:S(2)}) async-start(bf16[32,2,8,192]{3,2,1,0:T(8,128)(2,1)} %pad_maximum_fusion.1), calls=%async_computation.1 | async-start | bytes 524288 | tf_op jit(solution)/shard_map/all_to_all | solution.py:10
  103.0 9.1 %all-to-all-done.1 = bf16[32,2,8,192]{3,2,1,0:T(8,128)(2,1)S(1)} async-done(((bf16[32,2,8,192]{3,2,1,0:T(8,128)(2,1)}), bf16[32,2,8,192]{3,2,1,0:T(8,128)(2,1)S(1)}, u32[]{:S(2)}, u32[]{:S(2)}) %all-to-all-start.1) | async-done | bytes 196640 | tf_op jit(solution)/shard_map/all_to_all | solution.py:10
  112.1 0.6 broadcast_in_dim.13
  112.7 14.6 %all-to-all-start.5 = ((f32[16,1,256]{2,1,0:T(1,128)}), f32[16,1,256]{2,1,0:T(1,128)}, u32[]{:S(2)}, u32[]{:S(2)}) async-start(f32[16,1,256]{2,1,0:T(1,128)} %broadcast_in_dim.13), calls=%async_computation.5 | async-start | bytes 32768 | tf_op jit(solution)/shard_map/all_to_all | solution.py:14
  127.8 1.9 fusion.11
  129.7 0.7 fusion.2
  130.4 1.3 reshape.209
  131.8 3.0 %all-to-all-done.5 = f32[16,1,256]{2,1,0:T(1,128)} async-done(((f32[16,1,256]{2,1,0:T(1,128)}), f32[16,1,256]{2,1,0:T(1,128)}, u32[]{:S(2)}, u32[]{:S(2)}) %all-to-all-start.5) | async-done | bytes 16416 | tf_op jit(solution)/shard_map/all_to_all | solution.py:14
  134.7 4.4 %all-to-all-start.4 = ((f32[32,6,1536]{2,1,0:T(8,128)}), f32[32,6,1536]{2,1,0:T(8,128)S(1)}, u32[]{:S(2)}, u32[]{:S(2)}) async-start(f32[32,6,1536]{2,1,0:T(8,128)} %reshape.209), calls=%async_computation.4 | async-start | bytes 3145728 | tf_op jit(solution)/shard_map/all_to_all | solution.py:10
  139.9 0.3 copy.167
  140.3 1.5 copy.154
  141.8 33.9 %all-to-all-done.4 = f32[32,6,1536]{2,1,0:T(8,128)S(1)} async-done(((f32[32,6,1536]{2,1,0:T(8,128)}), f32[32,6,1536]{2,1,0:T(8,128)S(1)}, u32[]{:S(2)}, u32[]{:S(2)}) %all-to-all-start.4) | async-done | bytes 1179680 | tf_op jit(solution)/shard_map/all_to_all | solution.py:10
  175.7 7.7 %all-to-all-start.7 = ((f32[16,1,10240]{2,1,0:T(1,128)}), f32[16,1,10240]{2,1,0:T(1,128)S(1)}, u32[]{:S(2)}, u32[]{:S(2)}) async-start(f32[16,1,10240]{2,1,0:T(1,128)} %copy.154), calls=%async_computation.7 | async-start | bytes 1310720 | tf_op jit(solution)/shard_map/all_to_all | solution.py:14
  183.4 0.8 reduce_sum.38
  184.3 19.0 %all-to-all-done.7 = f32[16,1,10240]{2,1,0:T(1,128)S(1)} async-done(((f32[16,1,10240]{2,1,0:T(1,128)}), f32[16,1,10240]{2,1,0:T(1,128)S(1)}, u32[]{:S(2)}, u32[]{:S(2)}) %all-to-all-start.7) | async-done | bytes 655392 | tf_op jit(solution)/shard_map/all_to_all | solution.py:14
  203.3 1.7 broadcast_in_dim.14
  205.0 5.4 %all-to-all-start.6 = ((f32[32,1,9472]{2,1,0:T(1,128)}), f32[32,1,9472]{2,1,0:T(1,128)S(1)}, u32[]{:S(2)}, u32[]{:S(2)}) async-start(f32[32,1,9472]{2,1,0:T(1,128)} %broadcast_in_dim.14), calls=%async_computation.6 | async-start | bytes 2424832 | tf_op jit(solution)/shard_map/all_to_all | solution.py:10
  210.9 0.9 fusion.39
  211.8 0.4 reduce_sum.39
  212.3 0.6 reshape.216
  212.9 0.7 reshape.217
  213.6 28.2 %all-to-all-done.6 = f32[32,1,9472]{2,1,0:T(1,128)S(1)} async-done(((f32[32,1,9472]{2,1,0:T(1,128)}), f32[32,1,9472]{2,1,0:T(1,128)S(1)}, u32[]{:S(2)}, u32[]{:S(2)}) %all-to-all-start.6) | async-done | bytes 1212448 | tf_op jit(solution)/shard_map/all_to_all | solution.py:10
  242.1 0.9 slice.101
  243.0 0.9 slice.99
  243.9 0.9 fusion.38
  (122 shorter events, 6.7 us)
Async XLA Ops:
  0.6 49.4 %copy-start = (bf16[96,1536]{1,0:T(8,128)(2,1)S(1)}, bf16[96,1536]{1,0:T(8,128)(2,1)}, u32[]{:S(2)}) copy-start(bf16[96,1536]{1,0:T(8,128)(2,1)} %param.10) | copy-start | bytes 884740
  2.3 10.2 %collective-permute-start = (bf16[96,640]{1,0:T(8,128)(2,1)S(1)}, bf16[96,640]{1,0:T(8,128)(2,1)S(1)}, u32[]{:S(2)}, u32[]{:S(2)}) collective-permute-start(bf16[96,640]{1,0:T(8,128)(2,1)S(1)} %constant_dynamic-update-slice_fusion), channel_id=1, source_target_pairs={{0,1},{1,2},{2,3},{3,4},{4,5},{5,6},{6,7},{7,8},{8,9},{9,10},{10,1... | collective-permute-start | bytes 368648 | tf_op jit(solution)/shard_map/ppermute | solution.py:46
  5.8 6.7 %collective-permute-start.1 = (bf16[96,640]{1,0:T(8,128)(2,1)S(1)}, bf16[96,640]{1,0:T(8,128)(2,1)S(1)}, u32[]{:S(2)}, u32[]{:S(2)}) collective-permute-start(bf16[96,640]{1,0:T(8,128)(2,1)S(1)} %constant_dynamic-update-slice_fusion), channel_id=1, source_target_pairs={{0,15},{1,0},{2,1},{3,2},{4,3},{5,4},{6,5},{7,6},{8,7},{9,8},{10,9... | collective-permute-start | bytes 368648 | tf_op jit(solution)/shard_map/ppermute | solution.py:49
  12.5 4.0 %collective-permute-start.2 = (bf16[96,640]{1,0:T(8,128)(2,1)S(1)}, bf16[96,640]{1,0:T(8,128)(2,1)S(1)}, u32[]{:S(2)}, u32[]{:S(2)}) collective-permute-start(bf16[96,640]{1,0:T(8,128)(2,1)S(1)} %collective-permute-done), channel_id=1, source_target_pairs={{0,1},{1,2},{2,3},{3,4},{4,5},{5,6},{6,7},{7,8},{8,9},{9,10},{10,1... | collective-permute-start | bytes 368648 | tf_op jit(solution)/shard_map/ppermute | solution.py:46
  12.6 4.3 %collective-permute-start.3 = (bf16[96,640]{1,0:T(8,128)(2,1)S(1)}, bf16[96,640]{1,0:T(8,128)(2,1)S(1)}, u32[]{:S(2)}, u32[]{:S(2)}) collective-permute-start(bf16[96,640]{1,0:T(8,128)(2,1)S(1)} %collective-permute-done.1), channel_id=1, source_target_pairs={{0,15},{1,0},{2,1},{3,2},{4,3},{5,4},{6,5},{7,6},{8,7},{9,8},{10,9... | collective-permute-start | bytes 368648 | tf_op jit(solution)/shard_map/ppermute | solution.py:49
  16.5 5.5 %collective-permute-start.4 = (bf16[96,640]{1,0:T(8,128)(2,1)S(1)}, bf16[96,640]{1,0:T(8,128)(2,1)S(1)}, u32[]{:S(2)}, u32[]{:S(2)}) collective-permute-start(bf16[96,640]{1,0:T(8,128)(2,1)S(1)} %collective-permute-done.2), channel_id=1, source_target_pairs={{0,1},{1,2},{2,3},{3,4},{4,5},{5,6},{6,7},{7,8},{8,9},{9,10},{10,1... | collective-permute-start | bytes 368648 | tf_op jit(solution)/shard_map/ppermute | solution.py:46
  16.9 5.3 %collective-permute-start.5 = (bf16[96,640]{1,0:T(8,128)(2,1)S(1)}, bf16[96,640]{1,0:T(8,128)(2,1)S(1)}, u32[]{:S(2)}, u32[]{:S(2)}) collective-permute-start(bf16[96,640]{1,0:T(8,128)(2,1)S(1)} %collective-permute-done.3), channel_id=1, source_target_pairs={{0,15},{1,0},{2,1},{3,2},{4,3},{5,4},{6,5},{7,6},{8,7},{9,8},{10,9... | collective-permute-start | bytes 368648 | tf_op jit(solution)/shard_map/ppermute | solution.py:49
  22.0 5.5 %collective-permute-start.6 = (bf16[96,640]{1,0:T(8,128)(2,1)S(1)}, bf16[96,640]{1,0:T(8,128)(2,1)S(1)}, u32[]{:S(2)}, u32[]{:S(2)}) collective-permute-start(bf16[96,640]{1,0:T(8,128)(2,1)S(1)} %collective-permute-done.4), channel_id=1, source_target_pairs={{0,1},{1,2},{2,3},{3,4},{4,5},{5,6},{6,7},{7,8},{8,9},{9,10},{10,1... | collective-permute-start | bytes 368648 | tf_op jit(solution)/shard_map/ppermute | solution.py:46
  22.2 5.5 %collective-permute-start.7 = (bf16[96,640]{1,0:T(8,128)(2,1)S(1)}, bf16[96,640]{1,0:T(8,128)(2,1)S(1)}, u32[]{:S(2)}, u32[]{:S(2)}) collective-permute-start(bf16[96,640]{1,0:T(8,128)(2,1)S(1)} %collective-permute-done.5), channel_id=1, source_target_pairs={{0,15},{1,0},{2,1},{3,2},{4,3},{5,4},{6,5},{7,6},{8,7},{9,8},{10,9... | collective-permute-start | bytes 368648 | tf_op jit(solution)/shard_map/ppermute | solution.py:49
  27.5 5.5 %collective-permute-start.8 = (bf16[96,640]{1,0:T(8,128)(2,1)S(1)}, bf16[96,640]{1,0:T(8,128)(2,1)S(1)}, u32[]{:S(2)}, u32[]{:S(2)}) collective-permute-start(bf16[96,640]{1,0:T(8,128)(2,1)S(1)} %collective-permute-done.6), channel_id=1, source_target_pairs={{0,1},{1,2},{2,3},{3,4},{4,5},{5,6},{6,7},{7,8},{8,9},{9,10},{10,1... | collective-permute-start | bytes 368648 | tf_op jit(solution)/shard_map/ppermute | solution.py:46
  27.7 5.5 %collective-permute-start.9 = (bf16[96,640]{1,0:T(8,128)(2,1)S(1)}, bf16[96,640]{1,0:T(8,128)(2,1)S(1)}, u32[]{:S(2)}, u32[]{:S(2)}) collective-permute-start(bf16[96,640]{1,0:T(8,128)(2,1)S(1)} %collective-permute-done.7), channel_id=1, source_target_pairs={{0,15},{1,0},{2,1},{3,2},{4,3},{5,4},{6,5},{7,6},{8,7},{9,8},{10,9... | collective-permute-start | bytes 368648 | tf_op jit(solution)/shard_map/ppermute | solution.py:49
  32.3 17.8 %copy-start.15 = (bf16[96,512]{1,0:T(8,128)(2,1)S(1)}, bf16[96,512]{1,0:T(8,128)(2,1)}, u32[]{:S(2)}) copy-start(bf16[96,512]{1,0:T(8,128)(2,1)} %param.17) | copy-start | bytes 294916
  33.0 5.5 %collective-permute-start.10 = (bf16[96,640]{1,0:T(8,128)(2,1)S(1)}, bf16[96,640]{1,0:T(8,128)(2,1)S(1)}, u32[]{:S(2)}, u32[]{:S(2)}) collective-permute-start(bf16[96,640]{1,0:T(8,128)(2,1)S(1)} %collective-permute-done.8), channel_id=1, source_target_pairs={{0,1},{1,2},{2,3},{3,4},{4,5},{5,6},{6,7},{7,8},{8,9},{9,10},{10,1... | collective-permute-start | bytes 368648 | tf_op jit(solution)/shard_map/ppermute | solution.py:46
  33.2 5.5 %collective-permute-start.11 = (bf16[96,640]{1,0:T(8,128)(2,1)S(1)}, bf16[96,640]{1,0:T(8,128)(2,1)S(1)}, u32[]{:S(2)}, u32[]{:S(2)}) collective-permute-start(bf16[96,640]{1,0:T(8,128)(2,1)S(1)} %collective-permute-done.9), channel_id=1, source_target_pairs={{0,15},{1,0},{2,1},{3,2},{4,3},{5,4},{6,5},{7,6},{8,7},{9,8},{10,9... | collective-permute-start | bytes 368648 | tf_op jit(solution)/shard_map/ppermute | solution.py:49
  38.6 5.5 %collective-permute-start.12 = (bf16[96,640]{1,0:T(8,128)(2,1)S(1)}, bf16[96,640]{1,0:T(8,128)(2,1)S(1)}, u32[]{:S(2)}, u32[]{:S(2)}) collective-permute-start(bf16[96,640]{1,0:T(8,128)(2,1)S(1)} %collective-permute-done.10), channel_id=1, source_target_pairs={{0,1},{1,2},{2,3},{3,4},{4,5},{5,6},{6,7},{7,8},{8,9},{9,10},{10,1... | collective-permute-start | bytes 368648 | tf_op jit(solution)/shard_map/ppermute | solution.py:46
  38.7 5.5 %collective-permute-start.13 = (bf16[96,640]{1,0:T(8,128)(2,1)S(1)}, bf16[96,640]{1,0:T(8,128)(2,1)S(1)}, u32[]{:S(2)}, u32[]{:S(2)}) collective-permute-start(bf16[96,640]{1,0:T(8,128)(2,1)S(1)} %collective-permute-done.11), channel_id=1, source_target_pairs={{0,15},{1,0},{2,1},{3,2},{4,3},{5,4},{6,5},{7,6},{8,7},{9,8},{10,9... | collective-permute-start | bytes 368648 | tf_op jit(solution)/shard_map/ppermute | solution.py:49
  44.1 5.5 %collective-permute-start.14 = (bf16[96,640]{1,0:T(8,128)(2,1)S(1)}, bf16[96,640]{1,0:T(8,128)(2,1)S(1)}, u32[]{:S(2)}, u32[]{:S(2)}) collective-permute-start(bf16[96,640]{1,0:T(8,128)(2,1)S(1)} %collective-permute-done.12), channel_id=1, source_target_pairs={{0,1},{1,2},{2,3},{3,4},{4,5},{5,6},{6,7},{7,8},{8,9},{9,10},{10,1... | collective-permute-start | bytes 368648 | tf_op jit(solution)/shard_map/ppermute | solution.py:46
  50.5 0.7 copy-start.16
  50.5 13.0 %copy-start.7 = (bf16[2,256,256]{2,1,0:T(8,128)(2,1)S(1)}, bf16[2,256,256]{2,1,0:T(8,128)(2,1)}, u32[]{:S(2)}) copy-start(bf16[2,256,256]{2,1,0:T(8,128)(2,1)} %param.12) | copy-start | bytes 786436
  52.4 18.6 %all-to-all-start.2 = ((f32[32,1,640]{2,1,0:T(1,128)}), f32[32,1,640]{2,1,0:T(1,128)S(1)}, u32[]{:S(2)}, u32[]{:S(2)}) async-start(f32[32,1,640]{2,1,0:T(1,128)} %all_to_all.39), calls=%async_computation.2 | async-start | bytes 163840 | tf_op jit(solution)/shard_map/all_to_all | solution.py:10
  62.1 12.8 %copy-start.12 = (s32[64]{0:T(128)S(1)}, s32[64]{0:T(128)}, u32[]{:S(2)}) copy-start(s32[64]{0:T(128)} %param.16) | copy-start | bytes 772
  63.5 0.6 copy-start.9
  63.5 27.0 %copy-start.8 = (bf16[8,64,64]{2,1,0:T(8,128)(2,1)S(1)}, bf16[8,64,64]{2,1,0:T(8,128)(2,1)}, u32[]{:S(2)}) copy-start(bf16[8,64,64]{2,1,0:T(8,128)(2,1)} %param.13) | copy-start | bytes 196612
  71.0 13.5 %all-to-all-start = ((bf16[32,2,8,192]{3,2,1,0:T(8,128)(2,1)}), bf16[32,2,8,192]{3,2,1,0:T(8,128)(2,1)S(1)}, u32[]{:S(2)}, u32[]{:S(2)}) async-start(bf16[32,2,8,192]{3,2,1,0:T(8,128)(2,1)} %copy.133), calls=%async_computation | async-start | bytes 524288 | tf_op jit(solution)/shard_map/all_to_all | solution.py:10
  74.9 27.7 %copy-start.11 = (bf16[96,128]{1,0:T(8,128)(2,1)S(1)}, bf16[96,128]{1,0:T(8,128)(2,1)}, u32[]{:S(2)}) copy-start(bf16[96,128]{1,0:T(8,128)(2,1)} %param.15) | copy-start | bytes 73732
  74.9 0.5 copy-start.13
  85.2 13.3 %all-to-all-start.3 = ((f32[32,1,640]{2,1,0:T(1,128)}), f32[32,1,640]{2,1,0:T(1,128)S(1)}, u32[]{:S(2)}, u32[]{:S(2)}) async-start(f32[32,1,640]{2,1,0:T(1,128)} %broadcast_in_dim.11), calls=%async_computation.3 | async-start | bytes 163840 | tf_op jit(solution)/shard_map/all_to_all | solution.py:10
  89.8 0.6 copy-start.1
  90.0 0.7 copy-start.3
  98.6 13.5 %all-to-all-start.1 = ((bf16[32,2,8,192]{3,2,1,0:T(8,128)(2,1)}), bf16[32,2,8,192]{3,2,1,0:T(8,128)(2,1)S(1)}, u32[]{:S(2)}, u32[]{:S(2)}) async-start(bf16[32,2,8,192]{3,2,1,0:T(8,128)(2,1)} %pad_maximum_fusion.1), calls=%async_computation.1 | async-start | bytes 524288 | tf_op jit(solution)/shard_map/all_to_all | solution.py:10
  112.7 22.0 %all-to-all-start.5 = ((f32[16,1,256]{2,1,0:T(1,128)}), f32[16,1,256]{2,1,0:T(1,128)}, u32[]{:S(2)}, u32[]{:S(2)}) async-start(f32[16,1,256]{2,1,0:T(1,128)} %broadcast_in_dim.13), calls=%async_computation.5 | async-start | bytes 32768 | tf_op jit(solution)/shard_map/all_to_all | solution.py:14
  127.4 2.3 copy-start.5
  131.7 7.4 %copy-start.2 = (bf16[32,2,8,96]{3,1,0,2:T(2,128)(2,1)S(1)}, bf16[32,2,8,96]{3,1,0,2:T(2,128)(2,1)}, u32[]{:S(2)}) copy-start(bf16[32,2,8,96]{3,1,0,2:T(2,128)(2,1)} %copy-done.1) | copy-start | bytes 294916
  131.7 7.4 %copy-start.4 = (bf16[32,2,8,96]{3,1,0,2:T(2,128)(2,1)S(1)}, bf16[32,2,8,96]{3,1,0,2:T(2,128)(2,1)}, u32[]{:S(2)}) copy-start(bf16[32,2,8,96]{3,1,0,2:T(2,128)(2,1)} %copy-done.3) | copy-start | bytes 294916
  131.7 7.9 %copy-start.6 = (bf16[2,32,8,96]{3,2,0,1:T(8,128)(2,1)S(1)}, bf16[2,32,8,96]{3,2,0,1:T(8,128)(2,1)}, u32[]{:S(2)}) copy-start(bf16[2,32,8,96]{3,2,0,1:T(8,128)(2,1)} %copy-done.5) | copy-start | bytes 294916
  131.8 7.9 %copy-start.10 = (bf16[512,96]{0,1:T(8,128)(2,1)S(1)}, bf16[512,96]{0,1:T(8,128)(2,1)}, u32[]{:S(2)}) copy-start(bf16[512,96]{0,1:T(8,128)(2,1)} %copy-done.9) | copy-start | bytes 294916
  134.7 41.0 %all-to-all-start.4 = ((f32[32,6,1536]{2,1,0:T(8,128)}), f32[32,6,1536]{2,1,0:T(8,128)S(1)}, u32[]{:S(2)}, u32[]{:S(2)}) async-start(f32[32,6,1536]{2,1,0:T(8,128)} %reshape.209), calls=%async_computation.4 | async-start | bytes 3145728 | tf_op jit(solution)/shard_map/all_to_all | solution.py:10
  175.7 27.6 %all-to-all-start.7 = ((f32[16,1,10240]{2,1,0:T(1,128)}), f32[16,1,10240]{2,1,0:T(1,128)S(1)}, u32[]{:S(2)}, u32[]{:S(2)}) async-start(f32[16,1,10240]{2,1,0:T(1,128)} %copy.154), calls=%async_computation.7 | async-start | bytes 1310720 | tf_op jit(solution)/shard_map/all_to_all | solution.py:14
  184.3 26.1 %copy-start.14 = (f32[64]{0:T(128)S(1)}, f32[64]{0:T(128)}, u32[]{:S(2)}) copy-start(f32[64]{0:T(128)} %copy-done.13) | copy-start | bytes 772
  205.0 36.8 %all-to-all-start.6 = ((f32[32,1,9472]{2,1,0:T(1,128)}), f32[32,1,9472]{2,1,0:T(1,128)S(1)}, u32[]{:S(2)}, u32[]{:S(2)}) async-start(f32[32,1,9472]{2,1,0:T(1,128)} %broadcast_in_dim.14), calls=%async_computation.6 | async-start | bytes 2424832 | tf_op jit(solution)/shard_map/all_to_all | solution.py:10
